TPU v7x, 32 devices: a whole 2x2x4 slice. The times are simulated.
32 devices in a mesh: dom: 4 (over y, x), head: 8 (over z, core).
Axes of the slice: x: 2, y: 2, z: 4, core: 2. Of those that a mesh axis runs over, the one named last changes fastest.
Arguments:
- node_queries: bfloat16 [8192, 1024], P(('dom', 'head')), may hold values from -20 to 20
- node_keys: bfloat16 [8192, 1024], P(('dom', 'head')), may hold values from -20 to 20
- node_values: bfloat16 [8192, 1024], P(('dom', 'head')), may hold values from -6 to 6
- out_grad: bfloat16 [8192, 1024], P(('dom', 'head')), may hold values from -6 to 6
- degrees: int32 [8192], P('dom'), may hold values from 8 to 4096
- neighbor_blocks: int32 [64, 12], P('dom'), may hold values from 0 to 31, as said below
- send_slots: int32 [4, 4, 4], replicated, may hold values from -1 to 15, as said below
Outputs:
- grad_queries: bfloat16 [8192, 1024], P(('dom', 'head'))
- grad_keys: bfloat16 [8192, 1024], P(('dom', 'head'))
- grad_values: bfloat16 [8192, 1024], P(('dom', 'head'))
Inputs may be any that keep to these rules, and one draw needn't show every extreme that they name: `neighbor_blocks`: an entry t below 16 names block t of the row's own partition; entry 16 + q * 4 + s names slot s of send_slots[q, p] for the row's partition p, and that slot is live. The 12 entries of a row are distinct, and every live slot listed for a partition is named by some row block of it. send_slots[q, p] holds distinct local block numbers of partition q, live slots first and -1 in empty ones; send_slots[p, p] is empty; for every destination p at least one source fills all 4 slots, every other source fills 1 to 4.
All inputs are finite; a program needn't handle non-finite values.
Results may differ from a plain program's by a relative error of at most 0.0068.
Values may be sent and summed in bfloat16 or wider, within the bound.
No kernel may reach another device: no remote copies, remote signals or barrier semaphores. Data moves between devices by JAX's collectives and lax.ppermute only.
A program may use at most 128 MiB of HBM per device.

v0:
```python
import math
import jax
import jax.numpy as jnp
from jax import lax
from jax.sharding import PartitionSpec as P

D = 1024
H = 16
NBR = 12
BS = 128


def borrow_table(keys_h, values_h, my_lists, block):
    rows, width = keys_h.shape
    nblk = rows // block
    kv_local = jnp.concatenate([keys_h, values_h], 1).reshape(nblk, block, 2 * width)
    outgoing = jnp.take(kv_local, jnp.maximum(my_lists, 0).reshape(-1), axis=0)
    borrowed = lax.all_to_all(outgoing, "dom", split_axis=0, concat_axis=0, tiled=True)
    return jnp.concatenate([kv_local, borrowed], 0)


def body(node_queries, node_keys, node_values, out_grad, degrees, neighbor_blocks, send_slots):
    head_dim = D // H
    block = BS
    heads_here = H // lax.axis_size("head")
    parts = lax.axis_size("dom")
    my_lists = lax.dynamic_index_in_dim(send_slots, lax.axis_index("dom"), 0, keepdims=False)
    queries, keys_h, values_h, grads_h = (
        lax.all_to_all(node_queries, "head", split_axis=1, concat_axis=0, tiled=True),
        lax.all_to_all(node_keys, "head", split_axis=1, concat_axis=0, tiled=True),
        lax.all_to_all(node_values, "head", split_axis=1, concat_axis=0, tiled=True),
        lax.all_to_all(out_grad, "head", split_axis=1, concat_axis=0, tiled=True),
    )
    table = borrow_table(keys_h, values_h, my_lists, block)
    rows, width = queries.shape
    nblk = rows // block
    scale_rows = jnp.log(degrees.astype(jnp.float32)) / math.log(64.0) / math.sqrt(head_dim)
    group_rows = 4 * block
    span = NBR * block

    def group(acc, index):
        start = index * group_rows
        queries_g = lax.dynamic_slice_in_dim(queries, start, group_rows, 0).reshape(4, block, width)
        grads_g = lax.dynamic_slice_in_dim(grads_h, start, group_rows, 0).reshape(4, block, width)
        scale = lax.dynamic_slice_in_dim(scale_rows, start, group_rows, 0).reshape(4, block, 1)
        picks = lax.dynamic_slice_in_dim(neighbor_blocks, index * 4, 4, 0).reshape(-1)
        gathered = jnp.take(table, picks, axis=0).reshape(4, span, 2 * width)
        grad_q_heads = []
        grad_k_heads = []
        grad_v_heads = []
        for head in range(heads_here):
            low = head * head_dim
            keys_n = gathered[:, :, low : low + head_dim]
            values_n = gathered[:, :, width + low : width + low + head_dim]
            query_one = queries_g[:, :, low : low + head_dim]
            grad_one = grads_g[:, :, low : low + head_dim]
            scores = (
                jnp.einsum("gid,gjd->gij", query_one, keys_n, preferred_element_type=jnp.float32)
                * scale
            )
            top = jnp.max(scores, axis=-1, keepdims=True)
            expo = jnp.exp(scores - top)
            probs = expo / jnp.sum(expo, axis=-1, keepdims=True)
            dprobs = jnp.einsum(
                "gid,gjd->gij", grad_one, values_n, preferred_element_type=jnp.float32
            )
            delta = jnp.sum(probs * dprobs, axis=-1, keepdims=True)
            dscores = (probs * (dprobs - delta) * scale).astype(jnp.bfloat16)
            probs_b = probs.astype(jnp.bfloat16)
            grad_q_heads.append(
                jnp.einsum("gij,gjd->gid", dscores, keys_n, preferred_element_type=jnp.float32)
            )
            grad_k_heads.append(
                jnp.einsum("gij,gid->gjd", dscores, query_one, preferred_element_type=jnp.float32)
            )
            grad_v_heads.append(
                jnp.einsum("gij,gid->gjd", probs_b, grad_one, preferred_element_type=jnp.float32)
            )
        grad_q = jnp.concatenate(grad_q_heads, -1)
        contrib = jnp.concatenate(grad_k_heads + grad_v_heads, -1).reshape(
            4 * NBR, block, 2 * width
        )
        acc = acc.at[picks].add(contrib)
        return (acc, grad_q.reshape(group_rows, width).astype(jnp.bfloat16))

    acc0 = jnp.zeros((table.shape[0], block, 2 * width), jnp.float32)
    acc, grad_rows = lax.scan(group, acc0, jnp.arange(nblk // 4, dtype=jnp.int32))
    grad_queries_h = grad_rows.reshape(rows, width)
    remote = acc[nblk:].astype(jnp.bfloat16)
    returned = lax.all_to_all(remote, "dom", split_axis=0, concat_axis=0, tiled=True)
    targets = jnp.maximum(my_lists, 0).reshape(-1)
    onehot = (jnp.arange(nblk, dtype=jnp.int32)[:, None] == targets[None, :]).astype(jnp.bfloat16)
    added = jnp.dot(
        onehot, returned.reshape(parts * my_lists.shape[1], -1), preferred_element_type=jnp.float32
    )
    total = (acc[:nblk] + added.reshape(nblk, block, 2 * width)).astype(jnp.bfloat16)
    grad_keys_h = total[:, :, :width].reshape(rows, width)
    grad_values_h = total[:, :, width:].reshape(rows, width)
    grad_queries, grad_keys, grad_values = (
        lax.all_to_all(grad_queries_h, "head", split_axis=0, concat_axis=1, tiled=True),
        lax.all_to_all(grad_keys_h, "head", split_axis=0, concat_axis=1, tiled=True),
        lax.all_to_all(grad_values_h, "head", split_axis=0, concat_axis=1, tiled=True),
    )
    return (grad_queries, grad_keys, grad_values)


def solution(mesh):
    placed = (
        P(("dom", "head"), None),
        P(("dom", "head"), None),
        P(("dom", "head"), None),
        P(("dom", "head"), None),
        P("dom"),
        P("dom", None),
        P(),
    )
    return jax.shard_map(
        body,
        mesh=mesh,
        in_specs=placed,
        out_specs=(P(("dom", "head"), None), P(("dom", "head"), None), P(("dom", "head"), None)),
        check_vma=False,
    )
```

profile of v0, /device:TPU:0, one launch (start us, length us, event | category | flops | bytes accessed | tf_op | source)
XLA Modules:
  0.0 532.4 jit_solution(8709490764186849700)
XLA Ops:
  2.6 6.3 %all-to-all-start.1 = ((bf16[256,8,128]{2,0,1:T(8,128)(2,1)}), bf16[256,8,128]{2,0,1:T(8,128)(2,1)S(1)}, u32[]{:S(2)}, u32[]{:S(2)}) async-start(bf16[256,8,128]{2,0,1:T(8,128)(2,1)} %copy_bitcast_fusion.3), calls=%async_computation.1 | async-start | bytes 1048576 | tf_op jit(solution)/shard_map/all_to_all | solution.py:30
  10.8 13.4 %all-to-all-done.1 = bf16[256,8,128]{2,0,1:T(8,128)(2,1)S(1)} async-done(((bf16[256,8,128]{2,0,1:T(8,128)(2,1)}), bf16[256,8,128]{2,0,1:T(8,128)(2,1)S(1)}, u32[]{:S(2)}, u32[]{:S(2)}) %all-to-all-start.1) | async-done | bytes 524320 | tf_op jit(solution)/shard_map/all_to_all | solution.py:30
  24.3 3.5 all-to-all-start.2
  28.7 14.4 %all-to-all-done.2 = bf16[256,8,128]{2,0,1:T(8,128)(2,1)S(1)} async-done(((bf16[256,8,128]{2,0,1:T(8,128)(2,1)}), bf16[256,8,128]{2,0,1:T(8,128)(2,1)S(1)}, u32[]{:S(2)}, u32[]{:S(2)}) %all-to-all-start.2) | async-done | bytes 524320 | tf_op jit(solution)/shard_map/all_to_all | solution.py:31
  43.0 4.1 all-to-all-start
  50.4 12.2 %all-to-all-done = bf16[256,8,128]{2,0,1:T(8,128)(2,1)} async-done(((bf16[256,8,128]{2,0,1:T(8,128)(2,1)}), bf16[256,8,128]{2,0,1:T(8,128)(2,1)}, u32[]{:S(2)}, u32[]{:S(2)}) %all-to-all-start) | async-done | bytes 524320 | tf_op jit(solution)/shard_map/all_to_all | solution.py:29
  62.5 3.7 all-to-all-start.3
  67.2 12.6 %all-to-all-done.3 = bf16[16,128,256]{2,1,0:T(8,128)(2,1)S(1)} async-done(((bf16[16,128,256]{2,1,0:T(8,128)(2,1)}), bf16[16,128,256]{2,1,0:T(8,128)(2,1)S(1)}, u32[]{:S(2)}, u32[]{:S(2)}) %all-to-all-start.3) | async-done | bytes 1048608 | tf_op jit(solution)/shard_map/all_to_all | solution.py:18
  79.8 4.1 all-to-all-start.4
  85.4 13.9 %all-to-all-done.4 = bf16[256,8,128]{2,0,1:T(8,128)(2,1)} async-done(((bf16[256,8,128]{2,0,1:T(8,128)(2,1)}), bf16[256,8,128]{2,0,1:T(8,128)(2,1)}, u32[]{:S(2)}, u32[]{:S(2)}) %all-to-all-start.4) | async-done | bytes 524320 | tf_op jit(solution)/shard_map/all_to_all | solution.py:32
  101.7 354.8 %while.12 = (s32[]{:T(128)}, f32[32,128,256]{2,1,0:T(8,128)}, bf16[4,512,128]{2,1,0:T(8,128)(2,1)}, s32[4]{0:T(128)S(1)}, s32[16,12]{1,0:T(8,128)}, /*index=5*/b...) while((s32[]{:T(128)}, f32[32,128,256]{2,1,0:T(8,128)}, ...), condition=%wide.region_8.9_spmd, body=%wide.region_0.8_spmd.sunk | while | flops 1044722112 | bytes 177150128 | solution.py:87
  108.0 4.6 copy.120
  119.7 3.7 fusion.158
  123.5 7.1 %fusion.165 = bf16[4,128,64]{1,2,0:T(8,128)(2,1)S(1)} fusion(f32[4,128,1536]{2,1,0:T(8,128)} %fusion.162, f32[4,128]{1,0:T(4,128)S(1)} %dynamic-slice_bitcast_fusion.2, bf16[4,1536,256]{1,2,0:T(8,128)(2,1)} %copy-done.2, f32[4,128,1536]{2,1,0:T(8,128)} %get-tuple-element.159, f32[4,128]{1,0:T(4,128)S(1)} %get-tuple-element.160), kind=kOutput, calls=%fused_computation.41.clone.1 | convolution fusion | flops 106203136 | bytes 13441024 | tf_op jit(solution)/shard_map/while/body/eval_jaxpr/gij,gjd->gid/dot_general | solution.py:71
  130.6 8.5 %fusion.163 = f32[4,1536,64]{1,2,0:T(8,128)} fusion(f32[4,128,1536]{2,1,0:T(8,128)} %fusion.162, f32[4,128]{1,0:T(4,128)S(1)} %dynamic-slice_bitcast_fusion.2, bf16[4,128,128]{2,1,0:T(8,128)(2,1)S(1)} %bitcast.109, f32[4,128,1536]{2,1,0:T(8,128)} %get-tuple-element.159, f32[4,128]{1,0:T(4,128)S(1)} %get-tuple-element.160), kind=kOutput, calls=%fused_computation.30.clone.1 | convolution fusion | flops 106170368 | bytes 14292992 | tf_op jit(solution)/shard_map/while/body/eval_jaxpr/gij,gid->gjd/dot_general | solution.py:74
  139.0 3.5 fusion.159
  142.5 3.8 fusion.156
  146.3 7.2 %fusion.164 = bf16[4,128,64]{1,2,0:T(8,128)(2,1)S(1)} fusion(f32[4,128,1536]{2,1,0:T(8,128)} %fusion.160, f32[4,128]{1,0:T(4,128)S(1)} %dynamic-slice_bitcast_fusion.2, bf16[4,1536,256]{1,2,0:T(8,128)(2,1)} %copy-done.2, f32[4,128,1536]{2,1,0:T(8,128)} %get-tuple-element.157, f32[4,128]{1,0:T(4,128)S(1)} %get-tuple-element.158), kind=kOutput, calls=%fused_computation.42.clone.1 | convolution fusion | flops 106203136 | bytes 13441024 | tf_op jit(solution)/shard_map/while/body/eval_jaxpr/gij,gjd->gid/dot_general | solution.py:71
  153.5 8.6 %fusion.161 = f32[4,1536,64]{1,2,0:T(8,128)} fusion(f32[4,128,1536]{2,1,0:T(8,128)} %fusion.160, f32[4,128]{1,0:T(4,128)S(1)} %dynamic-slice_bitcast_fusion.2, bf16[4,128,128]{2,1,0:T(8,128)(2,1)S(1)} %bitcast.111, f32[4,128,1536]{2,1,0:T(8,128)} %get-tuple-element.157, f32[4,128]{1,0:T(4,128)S(1)} %get-tuple-element.158), kind=kOutput, calls=%fused_computation.28.clone.1 | convolution fusion | flops 106170368 | bytes 14292992 | tf_op jit(solution)/shard_map/while/body/eval_jaxpr/gij,gid->gjd/dot_general | solution.py:74
  162.1 2.6 fusion.157
  165.4 2.8 pad_maximum_fusion.6
  168.2 6.6 %copy.122 = f32[4,1536,256]{2,1,0:T(8,128)} copy(f32[4,1536,256]{1,2,0:T(8,128)} %pad_maximum_fusion.6) | data formatting | bytes 12582912 | tf_op jit(solution)/shard_map/while/body/eval_jaxpr/concatenate | solution.py:80
  174.8 14.8 %scatter_fusion = f32[32,128,256]{2,1,0:T(8,128)} fusion(f32[32,128,256]{2,1,0:T(8,128)} %get-tuple-element.177, s32[48]{0:T(128)S(1)} %fusion.155, f32[48,128,256]{2,1,0:T(8,128)} %bitcast.96), kind=kCustom, calls=%fused_computation.2.clone.1 | custom fusion | flops 1572864 | bytes 18874560 | tf_op jit(solution)/shard_map/while/body/eval_jaxpr/scatter-add | solution.py:83
  196.8 4.6 copy.120
  208.5 3.7 fusion.158
  212.2 7.1 %fusion.165 = bf16[4,128,64]{1,2,0:T(8,128)(2,1)S(1)} fusion(f32[4,128,1536]{2,1,0:T(8,128)} %fusion.162, f32[4,128]{1,0:T(4,128)S(1)} %dynamic-slice_bitcast_fusion.2, bf16[4,1536,256]{1,2,0:T(8,128)(2,1)} %copy-done.2, f32[4,128,1536]{2,1,0:T(8,128)} %get-tuple-element.159, f32[4,128]{1,0:T(4,128)S(1)} %get-tuple-element.160), kind=kOutput, calls=%fused_computation.41.clone.1 | convolution fusion | flops 106203136 | bytes 13441024 | tf_op jit(solution)/shard_map/while/body/eval_jaxpr/gij,gjd->gid/dot_general | solution.py:71
  219.3 8.5 %fusion.163 = f32[4,1536,64]{1,2,0:T(8,128)} fusion(f32[4,128,1536]{2,1,0:T(8,128)} %fusion.162, f32[4,128]{1,0:T(4,128)S(1)} %dynamic-slice_bitcast_fusion.2, bf16[4,128,128]{2,1,0:T(8,128)(2,1)S(1)} %bitcast.109, f32[4,128,1536]{2,1,0:T(8,128)} %get-tuple-element.159, f32[4,128]{1,0:T(4,128)S(1)} %get-tuple-element.160), kind=kOutput, calls=%fused_computation.30.clone.1 | convolution fusion | flops 106170368 | bytes 14292992 | tf_op jit(solution)/shard_map/while/body/eval_jaxpr/gij,gid->gjd/dot_general | solution.py:74
  227.7 3.5 fusion.159
  231.2 3.8 fusion.156
  235.0 7.2 %fusion.164 = bf16[4,128,64]{1,2,0:T(8,128)(2,1)S(1)} fusion(f32[4,128,1536]{2,1,0:T(8,128)} %fusion.160, f32[4,128]{1,0:T(4,128)S(1)} %dynamic-slice_bitcast_fusion.2, bf16[4,1536,256]{1,2,0:T(8,128)(2,1)} %copy-done.2, f32[4,128,1536]{2,1,0:T(8,128)} %get-tuple-element.157, f32[4,128]{1,0:T(4,128)S(1)} %get-tuple-element.158), kind=kOutput, calls=%fused_computation.42.clone.1 | convolution fusion | flops 106203136 | bytes 13441024 | tf_op jit(solution)/shard_map/while/body/eval_jaxpr/gij,gjd->gid/dot_general | solution.py:71
  242.2 8.6 %fusion.161 = f32[4,1536,64]{1,2,0:T(8,128)} fusion(f32[4,128,1536]{2,1,0:T(8,128)} %fusion.160, f32[4,128]{1,0:T(4,128)S(1)} %dynamic-slice_bitcast_fusion.2, bf16[4,128,128]{2,1,0:T(8,128)(2,1)S(1)} %bitcast.111, f32[4,128,1536]{2,1,0:T(8,128)} %get-tuple-element.157, f32[4,128]{1,0:T(4,128)S(1)} %get-tuple-element.158), kind=kOutput, calls=%fused_computation.28.clone.1 | convolution fusion | flops 106170368 | bytes 14292992 | tf_op jit(solution)/shard_map/while/body/eval_jaxpr/gij,gid->gjd/dot_general | solution.py:74
  254.1 2.8 pad_maximum_fusion.6
  256.9 6.6 %copy.122 = f32[4,1536,256]{2,1,0:T(8,128)} copy(f32[4,1536,256]{1,2,0:T(8,128)} %pad_maximum_fusion.6) | data formatting | bytes 12582912 | tf_op jit(solution)/shard_map/while/body/eval_jaxpr/concatenate | solution.py:80
  263.5 14.7 %scatter_fusion = f32[32,128,256]{2,1,0:T(8,128)} fusion(f32[32,128,256]{2,1,0:T(8,128)} %get-tuple-element.177, s32[48]{0:T(128)S(1)} %fusion.155, f32[48,128,256]{2,1,0:T(8,128)} %bitcast.96), kind=kCustom, calls=%fused_computation.2.clone.1 | custom fusion | flops 1572864 | bytes 18874560 | tf_op jit(solution)/shard_map/while/body/eval_jaxpr/scatter-add | solution.py:83
  285.4 4.6 copy.120
  297.1 3.7 fusion.158
  300.8 7.1 %fusion.165 = bf16[4,128,64]{1,2,0:T(8,128)(2,1)S(1)} fusion(f32[4,128,1536]{2,1,0:T(8,128)} %fusion.162, f32[4,128]{1,0:T(4,128)S(1)} %dynamic-slice_bitcast_fusion.2, bf16[4,1536,256]{1,2,0:T(8,128)(2,1)} %copy-done.2, f32[4,128,1536]{2,1,0:T(8,128)} %get-tuple-element.159, f32[4,128]{1,0:T(4,128)S(1)} %get-tuple-element.160), kind=kOutput, calls=%fused_computation.41.clone.1 | convolution fusion | flops 106203136 | bytes 13441024 | tf_op jit(solution)/shard_map/while/body/eval_jaxpr/gij,gjd->gid/dot_general | solution.py:71
  307.9 8.5 %fusion.163 = f32[4,1536,64]{1,2,0:T(8,128)} fusion(f32[4,128,1536]{2,1,0:T(8,128)} %fusion.162, f32[4,128]{1,0:T(4,128)S(1)} %dynamic-slice_bitcast_fusion.2, bf16[4,128,128]{2,1,0:T(8,128)(2,1)S(1)} %bitcast.109, f32[4,128,1536]{2,1,0:T(8,128)} %get-tuple-element.159, f32[4,128]{1,0:T(4,128)S(1)} %get-tuple-element.160), kind=kOutput, calls=%fused_computation.30.clone.1 | convolution fusion | flops 106170368 | bytes 14292992 | tf_op jit(solution)/shard_map/while/body/eval_jaxpr/gij,gid->gjd/dot_general | solution.py:74
  316.4 3.5 fusion.159
  319.9 3.8 fusion.156
  323.6 7.2 %fusion.164 = bf16[4,128,64]{1,2,0:T(8,128)(2,1)S(1)} fusion(f32[4,128,1536]{2,1,0:T(8,128)} %fusion.160, f32[4,128]{1,0:T(4,128)S(1)} %dynamic-slice_bitcast_fusion.2, bf16[4,1536,256]{1,2,0:T(8,128)(2,1)} %copy-done.2, f32[4,128,1536]{2,1,0:T(8,128)} %get-tuple-element.157, f32[4,128]{1,0:T(4,128)S(1)} %get-tuple-element.158), kind=kOutput, calls=%fused_computation.42.clone.1 | convolution fusion | flops 106203136 | bytes 13441024 | tf_op jit(solution)/shard_map/while/body/eval_jaxpr/gij,gjd->gid/dot_general | solution.py:71
  330.8 8.6 %fusion.161 = f32[4,1536,64]{1,2,0:T(8,128)} fusion(f32[4,128,1536]{2,1,0:T(8,128)} %fusion.160, f32[4,128]{1,0:T(4,128)S(1)} %dynamic-slice_bitcast_fusion.2, bf16[4,128,128]{2,1,0:T(8,128)(2,1)S(1)} %bitcast.111, f32[4,128,1536]{2,1,0:T(8,128)} %get-tuple-element.157, f32[4,128]{1,0:T(4,128)S(1)} %get-tuple-element.158), kind=kOutput, calls=%fused_computation.28.clone.1 | convolution fusion | flops 106170368 | bytes 14292992 | tf_op jit(solution)/shard_map/while/body/eval_jaxpr/gij,gid->gjd/dot_general | solution.py:74
  342.7 2.8 pad_maximum_fusion.6
  345.6 6.6 %copy.122 = f32[4,1536,256]{2,1,0:T(8,128)} copy(f32[4,1536,256]{1,2,0:T(8,128)} %pad_maximum_fusion.6) | data formatting | bytes 12582912 | tf_op jit(solution)/shard_map/while/body/eval_jaxpr/concatenate | solution.py:80
  352.1 14.8 %scatter_fusion = f32[32,128,256]{2,1,0:T(8,128)} fusion(f32[32,128,256]{2,1,0:T(8,128)} %get-tuple-element.177, s32[48]{0:T(128)S(1)} %fusion.155, f32[48,128,256]{2,1,0:T(8,128)} %bitcast.96), kind=kCustom, calls=%fused_computation.2.clone.1 | custom fusion | flops 1572864 | bytes 18874560 | tf_op jit(solution)/shard_map/while/body/eval_jaxpr/scatter-add | solution.py:83
  374.1 4.6 copy.120
  385.8 3.7 fusion.158
  389.5 7.1 %fusion.165 = bf16[4,128,64]{1,2,0:T(8,128)(2,1)S(1)} fusion(f32[4,128,1536]{2,1,0:T(8,128)} %fusion.162, f32[4,128]{1,0:T(4,128)S(1)} %dynamic-slice_bitcast_fusion.2, bf16[4,1536,256]{1,2,0:T(8,128)(2,1)} %copy-done.2, f32[4,128,1536]{2,1,0:T(8,128)} %get-tuple-element.159, f32[4,128]{1,0:T(4,128)S(1)} %get-tuple-element.160), kind=kOutput, calls=%fused_computation.41.clone.1 | convolution fusion | flops 106203136 | bytes 13441024 | tf_op jit(solution)/shard_map/while/body/eval_jaxpr/gij,gjd->gid/dot_general | solution.py:71
  396.6 8.5 %fusion.163 = f32[4,1536,64]{1,2,0:T(8,128)} fusion(f32[4,128,1536]{2,1,0:T(8,128)} %fusion.162, f32[4,128]{1,0:T(4,128)S(1)} %dynamic-slice_bitcast_fusion.2, bf16[4,128,128]{2,1,0:T(8,128)(2,1)S(1)} %bitcast.109, f32[4,128,1536]{2,1,0:T(8,128)} %get-tuple-element.159, f32[4,128]{1,0:T(4,128)S(1)} %get-tuple-element.160), kind=kOutput, calls=%fused_computation.30.clone.1 | convolution fusion | flops 106170368 | bytes 14292992 | tf_op jit(solution)/shard_map/while/body/eval_jaxpr/gij,gid->gjd/dot_general | solution.py:74
  405.1 3.5 fusion.159
  408.6 3.8 fusion.156
  412.4 7.2 %fusion.164 = bf16[4,128,64]{1,2,0:T(8,128)(2,1)S(1)} fusion(f32[4,128,1536]{2,1,0:T(8,128)} %fusion.160, f32[4,128]{1,0:T(4,128)S(1)} %dynamic-slice_bitcast_fusion.2, bf16[4,1536,256]{1,2,0:T(8,128)(2,1)} %copy-done.2, f32[4,128,1536]{2,1,0:T(8,128)} %get-tuple-element.157, f32[4,128]{1,0:T(4,128)S(1)} %get-tuple-element.158), kind=kOutput, calls=%fused_computation.42.clone.1 | convolution fusion | flops 106203136 | bytes 13441024 | tf_op jit(solution)/shard_map/while/body/eval_jaxpr/gij,gjd->gid/dot_general | solution.py:71
  419.5 8.6 %fusion.161 = f32[4,1536,64]{1,2,0:T(8,128)} fusion(f32[4,128,1536]{2,1,0:T(8,128)} %fusion.160, f32[4,128]{1,0:T(4,128)S(1)} %dynamic-slice_bitcast_fusion.2, bf16[4,128,128]{2,1,0:T(8,128)(2,1)S(1)} %bitcast.111, f32[4,128,1536]{2,1,0:T(8,128)} %get-tuple-element.157, f32[4,128]{1,0:T(4,128)S(1)} %get-tuple-element.158), kind=kOutput, calls=%fused_computation.28.clone.1 | convolution fusion | flops 106170368 | bytes 14292992 | tf_op jit(solution)/shard_map/while/body/eval_jaxpr/gij,gid->gjd/dot_general | solution.py:74
  431.4 2.8 pad_maximum_fusion.6
  434.3 6.6 %copy.122 = f32[4,1536,256]{2,1,0:T(8,128)} copy(f32[4,1536,256]{1,2,0:T(8,128)} %pad_maximum_fusion.6) | data formatting | bytes 12582912 | tf_op jit(solution)/shard_map/while/body/eval_jaxpr/concatenate | solution.py:80
  440.9 14.8 %scatter_fusion = f32[32,128,256]{2,1,0:T(8,128)} fusion(f32[32,128,256]{2,1,0:T(8,128)} %get-tuple-element.177, s32[48]{0:T(128)S(1)} %fusion.155, f32[48,128,256]{2,1,0:T(8,128)} %bitcast.96), kind=kCustom, calls=%fused_computation.2.clone.1 | custom fusion | flops 1572864 | bytes 18874560 | tf_op jit(solution)/shard_map/while/body/eval_jaxpr/scatter-add | solution.py:83
  458.2 16.6 %all_to_all.137 = bf16[16,128,256]{2,1,0:T(8,128)(2,1)S(1)} all-to-all(bf16[16,128,256]{2,1,0:T(8,128)(2,1)S(1)} %slice.107), channel_id=1, replica_groups=mesh['dom'=4,'head'=8] {'dom'}, dimensions={0} | all-to-all | bytes 2097152 | tf_op jit(solution)/shard_map/all_to_all | solution.py:90
  474.9 3.5 all-to-all-start.5
  478.4 4.6 copy.83
  484.9 8.8 %all-to-all-done.5 = bf16[8,256,128]{2,1,0:T(8,128)(2,1)S(1)} async-done(((bf16[8,256,128]{2,1,0:T(8,128)(2,1)}), bf16[8,256,128]{2,1,0:T(8,128)(2,1)S(1)}, u32[]{:S(2)}, u32[]{:S(2)}) %all-to-all-start.5) | async-done | bytes 524320 | tf_op jit(solution)/shard_map/all_to_all | solution.py:100
  493.6 3.5 all-to-all-start.8
  498.1 14.3 %all-to-all-done.8 = bf16[8,256,128]{2,1,0:T(8,128)(2,1)S(1)} async-done(((bf16[8,256,128]{2,1,0:T(8,128)(2,1)}), bf16[8,256,128]{2,1,0:T(8,128)(2,1)S(1)}, u32[]{:S(2)}, u32[]{:S(2)}) %all-to-all-start.8) | async-done | bytes 524320 | tf_op jit(solution)/shard_map/all_to_all | solution.py:102
  512.4 3.5 all-to-all-start.7
  518.4 12.8 %all-to-all-done.7 = bf16[8,256,128]{2,1,0:T(8,128)(2,1)S(1)} async-done(((bf16[8,256,128]{2,1,0:T(8,128)(2,1)}), bf16[8,256,128]{2,1,0:T(8,128)(2,1)S(1)}, u32[]{:S(2)}, u32[]{:S(2)}) %all-to-all-start.7) | async-done | bytes 524320 | tf_op jit(solution)/shard_map/all_to_all | solution.py:101
  (142 shorter events, 82.9 us)
Async XLA Ops:
  0.6 1.1 copy-start
  0.6 27.1 %copy-start.7 = (bf16[256,1024]{1,0:T(8,128)(2,1)S(1)}, bf16[256,1024]{1,0:T(8,128)(2,1)}, u32[]{:S(2)}) copy-start(bf16[256,1024]{1,0:T(8,128)(2,1)} %param.9) | copy-start | bytes 1572868
  2.6 21.7 %all-to-all-start.1 = ((bf16[256,8,128]{2,0,1:T(8,128)(2,1)}), bf16[256,8,128]{2,0,1:T(8,128)(2,1)S(1)}, u32[]{:S(2)}, u32[]{:S(2)}) async-start(bf16[256,8,128]{2,0,1:T(8,128)(2,1)} %copy_bitcast_fusion.3), calls=%async_computation.1 | async-start | bytes 1048576 | tf_op jit(solution)/shard_map/all_to_all | solution.py:30
  24.3 18.8 %all-to-all-start.2 = ((bf16[256,8,128]{2,0,1:T(8,128)(2,1)}), bf16[256,8,128]{2,0,1:T(8,128)(2,1)S(1)}, u32[]{:S(2)}, u32[]{:S(2)}) async-start(bf16[256,8,128]{2,0,1:T(8,128)(2,1)} %copy_bitcast_fusion.2), calls=%async_computation.2 | async-start | bytes 1048576 | tf_op jit(solution)/shard_map/all_to_all | solution.py:31
  43.0 19.5 %all-to-all-start = ((bf16[256,8,128]{2,0,1:T(8,128)(2,1)}), bf16[256,8,128]{2,0,1:T(8,128)(2,1)}, u32[]{:S(2)}, u32[]{:S(2)}) async-start(bf16[256,8,128]{2,0,1:T(8,128)(2,1)} %copy_bitcast_fusion.4), calls=%async_computation | async-start | bytes 1048576 | tf_op jit(solution)/shard_map/all_to_all | solution.py:29
  48.0 0.5 copy-start.10
  49.2 17.1 %copy-start.8 = (bf16[256,1024]{1,0:T(8,128)(2,1)S(1)}, bf16[256,1024]{1,0:T(8,128)(2,1)}, u32[]{:S(2)}) copy-start(bf16[256,1024]{1,0:T(8,128)(2,1)} %param.12) | copy-start | bytes 1572868
  49.2 34.7 %copy-start.9 = (s32[2048]{0:T(1024)S(1)}, s32[2048]{0:T(1024)}, u32[]{:S(2)}) copy-start(s32[2048]{0:T(1024)} %param.13) | copy-start | bytes 24580
  62.5 17.2 %all-to-all-start.3 = ((bf16[16,128,256]{2,1,0:T(8,128)(2,1)}), bf16[16,128,256]{2,1,0:T(8,128)(2,1)S(1)}, u32[]{:S(2)}, u32[]{:S(2)}) async-start(bf16[16,128,256]{2,1,0:T(8,128)(2,1)} %broadcast_select_fusion.1), calls=%async_computation.3 | async-start | bytes 2097152 | tf_op jit(solution)/shard_map/all_to_all | solution.py:18
  79.7 4.2 copy-start.6
  79.8 19.5 %all-to-all-start.4 = ((bf16[256,8,128]{2,0,1:T(8,128)(2,1)}), bf16[256,8,128]{2,0,1:T(8,128)(2,1)}, u32[]{:S(2)}, u32[]{:S(2)}) async-start(bf16[256,8,128]{2,0,1:T(8,128)(2,1)} %copy_bitcast_fusion.1), calls=%async_computation.4 | async-start | bytes 1048576 | tf_op jit(solution)/shard_map/all_to_all | solution.py:32
  114.9 2.6 copy-start.2
  162.1 2.6 copy-start.3
  162.1 2.8 copy-start.4
  162.1 3.3 copy-start.5
  203.6 2.6 copy-start.2
  250.8 2.6 copy-start.3
  250.8 2.8 copy-start.4
  250.8 3.3 copy-start.5
  292.2 2.6 copy-start.2
  339.4 2.6 copy-start.3
  339.4 2.8 copy-start.4
  339.4 3.3 copy-start.5
  380.9 2.6 copy-start.2
  428.1 2.6 copy-start.3
  428.1 2.8 copy-start.4
  428.1 3.3 copy-start.5
  474.9 18.8 %all-to-all-start.5 = ((bf16[8,256,128]{2,1,0:T(8,128)(2,1)}), bf16[8,256,128]{2,1,0:T(8,128)(2,1)S(1)}, u32[]{:S(2)}, u32[]{:S(2)}) async-start(bf16[8,256,128]{2,1,0:T(8,128)(2,1)} %bitcast.17), calls=%async_computation.5 | async-start | bytes 1048576 | tf_op jit(solution)/shard_map/all_to_all | solution.py:100
  478.4 4.6 copy-start.11
  493.6 18.8 %all-to-all-start.8 = ((bf16[8,256,128]{2,1,0:T(8,128)(2,1)}), bf16[8,256,128]{2,1,0:T(8,128)(2,1)S(1)}, u32[]{:S(2)}, u32[]{:S(2)}) async-start(bf16[8,256,128]{2,1,0:T(8,128)(2,1)} %bitcast.25), calls=%async_computation.8 | async-start | bytes 1048576 | tf_op jit(solution)/shard_map/all_to_all | solution.py:102
  512.4 18.8 %all-to-all-start.7 = ((bf16[8,256,128]{2,1,0:T(8,128)(2,1)}), bf16[8,256,128]{2,1,0:T(8,128)(2,1)S(1)}, u32[]{:S(2)}, u32[]{:S(2)}) async-start(bf16[8,256,128]{2,1,0:T(8,128)(2,1)} %bitcast.22), calls=%async_computation.7 | async-start | bytes 1048576 | tf_op jit(solution)/shard_map/all_to_all | solution.py:101
  515.9 16.5 %copy-start.1 = (bf16[256,1024]{1,0:T(8,128)(2,1)S(1)}, bf16[256,1024]{1,0:T(8,128)(2,1)}, u32[]{:S(2)}) copy-start(bf16[256,1024]{1,0:T(8,128)(2,1)} %param.10) | copy-start | bytes 1572868
where the time goes:
time: 535 us; the launch traced here: 532 us
  matrix products  200 us (37%)
  waiting for transfers between devices  102 us (19%)
  local copies, waits for them, and re-layouts  89.5 us (17%)
  other arithmetic  85.4 us (16%)
  starting transfers between devices  32.3 us (6%)
  blocking collectives  16.6 us (3%)
  loops' own time  5.52 us (1%)
    dot_general x8, matrix products, group(): jnp.einsum('gij,gid->gjd', dscores, query_one, preferred_element_type=jnp...  68.3 us
    scatter-add x4, other arithmetic, group(): acc = acc.at[picks].add(contrib)  59 us
    dot_general x8, matrix products, group(): jnp.einsum('gij,gjd->gid', dscores, keys_n, preferred_element_type=jnp.fl...  57 us
    sub x8, matrix products, group(): expo = jnp.exp(scores - top)  29.9 us
    gather x8, local copies, waits for them, and re-layouts, group(): gathered = jnp.take(table, picks, axis=0).reshape(4, span, 2 * width)  28.6 us
    concatenate x4, local copies, waits for them, and re-layouts, group(): jnp.concatenate(grad_k_heads + grad_v_heads, -1)  26.3 us
    dot_general x8, matrix products, group(): jnp.einsum('gij,gid->gjd', probs_b, grad_one, preferred_element_type=jnp....  24.4 us
    dot_general x8, matrix products, group(): jnp.einsum('gid,gjd->gij', grad_one, values_n, preferred_element_type=jnp...  19.4 us
  transfers between devices with their start and end apart: 8, of which 8 were waited for; matrix products, arithmetic and copies ran while one was open for 3% of the time, Pallas kernels for 0%

commit v1 on v0

--- a/solution.py
+++ b/solution.py
@@ -8,6 +8,20 @@
 H = 16
 NBR = 12
 BS = 128
+
+
+def spans_put(original, dim_no, values):
+    wide_out = original.shape
+    piece_next = original.reshape(
+        *wide_out[:dim_no], values, wide_out[dim_no] // values, *wide_out[dim_no + 1 :]
+    )
+    return jnp.moveaxis(piece_next, dim_no, 0)
+
+
+def _derive_classes(matrix, dim_k):
+    kept_arr = list(matrix.shape[1:])
+    kept_arr[dim_k] *= matrix.shape[0]
+    return jnp.moveaxis(matrix, 0, dim_k).reshape(kept_arr)
 
 
 def borrow_table(keys_h, values_h, my_lists, block):
@@ -25,11 +39,26 @@
     heads_here = H // lax.axis_size("head")
     parts = lax.axis_size("dom")
     my_lists = lax.dynamic_index_in_dim(send_slots, lax.axis_index("dom"), 0, keepdims=False)
+
+    def create_leaf(inp, ax_name, my_tile, local_array):
+        item_now, t_next = (jax.lax.axis_size(ax_name), jax.lax.axis_index(ax_name))
+        local_now = spans_put(inp, my_tile, item_now)
+        gallery = [local_now[t_next]]
+        rr = 1
+        while rr < item_now:
+            a_next = local_now[t_next ^ rr]
+            gallery.append(
+                jax.lax.ppermute(a_next, ax_name, [(h, h ^ rr) for h in range(item_now)])
+            )
+            rr += 1
+        local_now = jnp.stack(gallery)[t_next ^ jnp.arange(item_now)]
+        return _derive_classes(local_now, local_array)
+
     queries, keys_h, values_h, grads_h = (
         lax.all_to_all(node_queries, "head", split_axis=1, concat_axis=0, tiled=True),
         lax.all_to_all(node_keys, "head", split_axis=1, concat_axis=0, tiled=True),
         lax.all_to_all(node_values, "head", split_axis=1, concat_axis=0, tiled=True),
-        lax.all_to_all(out_grad, "head", split_axis=1, concat_axis=0, tiled=True),
+        create_leaf(out_grad, "head", 1, 0),
     )
     table = borrow_table(keys_h, values_h, my_lists, block)
     rows, width = queries.shape

time: 535 us -> 519 us (0.970)
  waiting for transfers between devices: 102 us -> 73.6 us
  local copies, waits for them, and re-layouts: 89.5 us -> 95.9 us
    all_to_all x1 -> x0, waiting for transfers between devices: 13.9 us -> none  [body(): lax.all_to_all(out_grad, 'head', split_axis=1, concat_axis=0, tiled=True)]
    all_to_all x1, waiting for transfers between devices: 13.4 us -> 3.15 us  [body(): lax.all_to_all(node_keys, 'head', split_axis=1, concat_axis=0, tiled=True)]
    ppermute x0 -> x7, starting transfers between devices: none -> 7.82 us  [create_leaf(): jax.lax.ppermute(a_next, ax_name, [(h, h ^ rr) for h in range(item_now)])]
  transfers between devices with their start and end apart: 8 -> 14, of which waited for: 8 -> 7; matrix products, arithmetic and copies ran while one was open for 3% -> 5% of each run, Pallas kernels for 0% -> 0%
where the time goes in v1:
time: 519 us; the launch traced here: 517 us
  matrix products  200 us (39%)
  local copies, waits for them, and re-layouts  95.9 us (18%)
  other arithmetic  87.3 us (17%)
  waiting for transfers between devices  73.6 us (14%)
  starting transfers between devices  36.1 us (7%)
  blocking collectives  16.7 us (3%)
  loops' own time  5.52 us (1%)
    dot_general x8, matrix products, group(): jnp.einsum('gij,gid->gjd', dscores, query_one, preferred_element_type=jnp...  68.7 us
    scatter-add x4, other arithmetic, group(): acc = acc.at[picks].add(contrib)  59.2 us
    dot_general x8, matrix products, group(): jnp.einsum('gij,gjd->gid', dscores, keys_n, preferred_element_type=jnp.fl...  57.3 us
    sub x8, matrix products, group(): expo = jnp.exp(scores - top)  29.9 us
    gather x8, local copies, waits for them, and re-layouts, group(): gathered = jnp.take(table, picks, axis=0).reshape(4, span, 2 * width)  28.7 us
    concatenate x4, local copies, waits for them, and re-layouts, group(): jnp.concatenate(grad_k_heads + grad_v_heads, -1)  26.4 us
    dot_general x8, matrix products, group(): jnp.einsum('gij,gid->gjd', probs_b, grad_one, preferred_element_type=jnp....  24.3 us
    dot_general x8, matrix products, group(): jnp.einsum('gid,gjd->gij', grad_one, values_n, preferred_element_type=jnp...  19.4 us
  transfers between devices with their start and end apart: 14, of which 7 were waited for; matrix products, arithmetic and copies ran while one was open for 5% of the time, Pallas kernels for 0%

profile of v1, /device:TPU:0, one launch (start us, length us, event | category | flops | bytes accessed | tf_op | source)
XLA Modules:
  0.0 516.6 jit_solution(14559993226707248072)
XLA Ops:
  2.6 6.5 %all-to-all-start.1 = ((bf16[256,8,128]{2,0,1:T(8,128)(2,1)}), bf16[256,8,128]{2,0,1:T(8,128)(2,1)S(1)}, u32[]{:S(2)}, u32[]{:S(2)}) async-start(bf16[256,8,128]{2,0,1:T(8,128)(2,1)} %copy_bitcast_fusion.2), calls=%async_computation.1 | async-start | bytes 1048576 | tf_op jit(solution)/shard_map/all_to_all | solution.py:59
  14.3 2.6 collective-permute-start.3
  21.7 3.2 all-to-all-done.1
  24.9 3.5 all-to-all-start.2
  30.5 13.1 %all-to-all-done.2 = bf16[256,8,128]{2,0,1:T(8,128)(2,1)S(1)} async-done(((bf16[256,8,128]{2,0,1:T(8,128)(2,1)}), bf16[256,8,128]{2,0,1:T(8,128)(2,1)S(1)}, u32[]{:S(2)}, u32[]{:S(2)}) %all-to-all-start.2) | async-done | bytes 524320 | tf_op jit(solution)/shard_map/all_to_all | solution.py:60
  45.7 3.7 all-to-all-start.3
  54.0 9.0 %all-to-all-done.3 = bf16[16,128,256]{2,1,0:T(8,128)(2,1)S(1)} async-done(((bf16[16,128,256]{2,1,0:T(8,128)(2,1)}), bf16[16,128,256]{2,1,0:T(8,128)(2,1)S(1)}, u32[]{:S(2)}, u32[]{:S(2)}) %all-to-all-start.3) | async-done | bytes 1048608 | tf_op jit(solution)/shard_map/all_to_all | solution.py:32
  62.9 4.2 all-to-all-start
  70.1 12.4 %all-to-all-done = bf16[256,8,128]{2,0,1:T(8,128)(2,1)} async-done(((bf16[256,8,128]{2,0,1:T(8,128)(2,1)}), bf16[256,8,128]{2,0,1:T(8,128)(2,1)}, u32[]{:S(2)}, u32[]{:S(2)}) %all-to-all-start) | async-done | bytes 524320 | tf_op jit(solution)/shard_map/all_to_all | solution.py:58
  84.9 355.7 %while.12 = (s32[]{:T(128)}, f32[32,128,256]{2,1,0:T(8,128)}, bf16[4,512,128]{2,1,0:T(8,128)(2,1)}, s32[4]{0:T(128)S(1)}, s32[16,12]{1,0:T(8,128)}, /*index=5*/b...) while((s32[]{:T(128)}, f32[32,128,256]{2,1,0:T(8,128)}, ...), condition=%wide.region_8.9_spmd, body=%wide.region_0.8_spmd.sunk | while | flops 1044722112 | bytes 177150128 | solution.py:116
  91.2 4.7 copy.140
  103.0 3.7 fusion.159
  106.7 7.1 %fusion.166 = bf16[4,128,64]{1,2,0:T(8,128)(2,1)S(1)} fusion(f32[4,128,1536]{2,1,0:T(8,128)} %fusion.163, f32[4,128]{1,0:T(4,128)S(1)} %dynamic-slice_bitcast_fusion.2, bf16[4,1536,256]{1,2,0:T(8,128)(2,1)} %copy-done.2, f32[4,128,1536]{2,1,0:T(8,128)} %get-tuple-element.167, f32[4,128]{1,0:T(4,128)S(1)} %get-tuple-element.168), kind=kOutput, calls=%fused_computation.42.clone.1 | convolution fusion | flops 106203136 | bytes 13441024 | tf_op jit(solution)/shard_map/while/body/eval_jaxpr/gij,gjd->gid/dot_general | solution.py:100
  113.8 8.5 %fusion.164 = f32[4,1536,64]{1,2,0:T(8,128)} fusion(f32[4,128,1536]{2,1,0:T(8,128)} %fusion.163, f32[4,128]{1,0:T(4,128)S(1)} %dynamic-slice_bitcast_fusion.2, bf16[4,128,128]{2,1,0:T(8,128)(2,1)S(1)} %bitcast.128, f32[4,128,1536]{2,1,0:T(8,128)} %get-tuple-element.167, f32[4,128]{1,0:T(4,128)S(1)} %get-tuple-element.168), kind=kOutput, calls=%fused_computation.31.clone.1 | convolution fusion | flops 106170368 | bytes 14292992 | tf_op jit(solution)/shard_map/while/body/eval_jaxpr/gij,gid->gjd/dot_general | solution.py:103
  122.3 3.5 fusion.160
  125.8 3.8 fusion.157
  129.5 7.2 %fusion.165 = bf16[4,128,64]{1,2,0:T(8,128)(2,1)S(1)} fusion(f32[4,128,1536]{2,1,0:T(8,128)} %fusion.161, f32[4,128]{1,0:T(4,128)S(1)} %dynamic-slice_bitcast_fusion.2, bf16[4,1536,256]{1,2,0:T(8,128)(2,1)} %copy-done.2, f32[4,128,1536]{2,1,0:T(8,128)} %get-tuple-element.165, f32[4,128]{1,0:T(4,128)S(1)} %get-tuple-element.166), kind=kOutput, calls=%fused_computation.43.clone.1 | convolution fusion | flops 106203136 | bytes 13441024 | tf_op jit(solution)/shard_map/while/body/eval_jaxpr/gij,gjd->gid/dot_general | solution.py:100
  136.8 8.7 %fusion.162 = f32[4,1536,64]{1,2,0:T(8,128)} fusion(f32[4,128,1536]{2,1,0:T(8,128)} %fusion.161, f32[4,128]{1,0:T(4,128)S(1)} %dynamic-slice_bitcast_fusion.2, bf16[4,128,128]{2,1,0:T(8,128)(2,1)S(1)} %bitcast.130, f32[4,128,1536]{2,1,0:T(8,128)} %get-tuple-element.165, f32[4,128]{1,0:T(4,128)S(1)} %get-tuple-element.166), kind=kOutput, calls=%fused_computation.29.clone.1 | convolution fusion | flops 106170368 | bytes 14292992 | tf_op jit(solution)/shard_map/while/body/eval_jaxpr/gij,gid->gjd/dot_general | solution.py:103
  145.5 2.6 fusion.158
  148.8 2.8 pad_maximum_fusion.6
  151.6 6.6 %copy.142 = f32[4,1536,256]{2,1,0:T(8,128)} copy(f32[4,1536,256]{1,2,0:T(8,128)} %pad_maximum_fusion.6) | data formatting | bytes 12582912 | tf_op jit(solution)/shard_map/while/body/eval_jaxpr/concatenate | solution.py:109
  158.2 14.9 %scatter_fusion = f32[32,128,256]{2,1,0:T(8,128)} fusion(f32[32,128,256]{2,1,0:T(8,128)} %get-tuple-element.185, s32[48]{0:T(128)S(1)} %fusion.156, f32[48,128,256]{2,1,0:T(8,128)} %bitcast.115), kind=kCustom, calls=%fused_computation.3.clone.1 | custom fusion | flops 1572864 | bytes 18874560 | tf_op jit(solution)/shard_map/while/body/eval_jaxpr/scatter-add | solution.py:112
  180.2 4.7 copy.140
  192.0 3.7 fusion.159
  195.7 7.1 %fusion.166 = bf16[4,128,64]{1,2,0:T(8,128)(2,1)S(1)} fusion(f32[4,128,1536]{2,1,0:T(8,128)} %fusion.163, f32[4,128]{1,0:T(4,128)S(1)} %dynamic-slice_bitcast_fusion.2, bf16[4,1536,256]{1,2,0:T(8,128)(2,1)} %copy-done.2, f32[4,128,1536]{2,1,0:T(8,128)} %get-tuple-element.167, f32[4,128]{1,0:T(4,128)S(1)} %get-tuple-element.168), kind=kOutput, calls=%fused_computation.42.clone.1 | convolution fusion | flops 106203136 | bytes 13441024 | tf_op jit(solution)/shard_map/while/body/eval_jaxpr/gij,gjd->gid/dot_general | solution.py:100
  202.8 8.5 %fusion.164 = f32[4,1536,64]{1,2,0:T(8,128)} fusion(f32[4,128,1536]{2,1,0:T(8,128)} %fusion.163, f32[4,128]{1,0:T(4,128)S(1)} %dynamic-slice_bitcast_fusion.2, bf16[4,128,128]{2,1,0:T(8,128)(2,1)S(1)} %bitcast.128, f32[4,128,1536]{2,1,0:T(8,128)} %get-tuple-element.167, f32[4,128]{1,0:T(4,128)S(1)} %get-tuple-element.168), kind=kOutput, calls=%fused_computation.31.clone.1 | convolution fusion | flops 106170368 | bytes 14292992 | tf_op jit(solution)/shard_map/while/body/eval_jaxpr/gij,gid->gjd/dot_general | solution.py:103
  211.3 3.5 fusion.160
  214.8 3.8 fusion.157
  218.5 7.2 %fusion.165 = bf16[4,128,64]{1,2,0:T(8,128)(2,1)S(1)} fusion(f32[4,128,1536]{2,1,0:T(8,128)} %fusion.161, f32[4,128]{1,0:T(4,128)S(1)} %dynamic-slice_bitcast_fusion.2, bf16[4,1536,256]{1,2,0:T(8,128)(2,1)} %copy-done.2, f32[4,128,1536]{2,1,0:T(8,128)} %get-tuple-element.165, f32[4,128]{1,0:T(4,128)S(1)} %get-tuple-element.166), kind=kOutput, calls=%fused_computation.43.clone.1 | convolution fusion | flops 106203136 | bytes 13441024 | tf_op jit(solution)/shard_map/while/body/eval_jaxpr/gij,gjd->gid/dot_general | solution.py:100
  225.8 8.7 %fusion.162 = f32[4,1536,64]{1,2,0:T(8,128)} fusion(f32[4,128,1536]{2,1,0:T(8,128)} %fusion.161, f32[4,128]{1,0:T(4,128)S(1)} %dynamic-slice_bitcast_fusion.2, bf16[4,128,128]{2,1,0:T(8,128)(2,1)S(1)} %bitcast.130, f32[4,128,1536]{2,1,0:T(8,128)} %get-tuple-element.165, f32[4,128]{1,0:T(4,128)S(1)} %get-tuple-element.166), kind=kOutput, calls=%fused_computation.29.clone.1 | convolution fusion | flops 106170368 | bytes 14292992 | tf_op jit(solution)/shard_map/while/body/eval_jaxpr/gij,gid->gjd/dot_general | solution.py:103
  234.5 2.6 fusion.158
  237.8 2.8 pad_maximum_fusion.6
  240.6 6.6 %copy.142 = f32[4,1536,256]{2,1,0:T(8,128)} copy(f32[4,1536,256]{1,2,0:T(8,128)} %pad_maximum_fusion.6) | data formatting | bytes 12582912 | tf_op jit(solution)/shard_map/while/body/eval_jaxpr/concatenate | solution.py:109
  247.2 14.7 %scatter_fusion = f32[32,128,256]{2,1,0:T(8,128)} fusion(f32[32,128,256]{2,1,0:T(8,128)} %get-tuple-element.185, s32[48]{0:T(128)S(1)} %fusion.156, f32[48,128,256]{2,1,0:T(8,128)} %bitcast.115), kind=kCustom, calls=%fused_computation.3.clone.1 | custom fusion | flops 1572864 | bytes 18874560 | tf_op jit(solution)/shard_map/while/body/eval_jaxpr/scatter-add | solution.py:112
  269.1 4.7 copy.140
  280.8 3.7 fusion.159
  284.5 7.1 %fusion.166 = bf16[4,128,64]{1,2,0:T(8,128)(2,1)S(1)} fusion(f32[4,128,1536]{2,1,0:T(8,128)} %fusion.163, f32[4,128]{1,0:T(4,128)S(1)} %dynamic-slice_bitcast_fusion.2, bf16[4,1536,256]{1,2,0:T(8,128)(2,1)} %copy-done.2, f32[4,128,1536]{2,1,0:T(8,128)} %get-tuple-element.167, f32[4,128]{1,0:T(4,128)S(1)} %get-tuple-element.168), kind=kOutput, calls=%fused_computation.42.clone.1 | convolution fusion | flops 106203136 | bytes 13441024 | tf_op jit(solution)/shard_map/while/body/eval_jaxpr/gij,gjd->gid/dot_general | solution.py:100
  291.6 8.5 %fusion.164 = f32[4,1536,64]{1,2,0:T(8,128)} fusion(f32[4,128,1536]{2,1,0:T(8,128)} %fusion.163, f32[4,128]{1,0:T(4,128)S(1)} %dynamic-slice_bitcast_fusion.2, bf16[4,128,128]{2,1,0:T(8,128)(2,1)S(1)} %bitcast.128, f32[4,128,1536]{2,1,0:T(8,128)} %get-tuple-element.167, f32[4,128]{1,0:T(4,128)S(1)} %get-tuple-element.168), kind=kOutput, calls=%fused_computation.31.clone.1 | convolution fusion | flops 106170368 | bytes 14292992 | tf_op jit(solution)/shard_map/while/body/eval_jaxpr/gij,gid->gjd/dot_general | solution.py:103
  300.1 3.5 fusion.160
  303.6 3.8 fusion.157
  307.4 7.2 %fusion.165 = bf16[4,128,64]{1,2,0:T(8,128)(2,1)S(1)} fusion(f32[4,128,1536]{2,1,0:T(8,128)} %fusion.161, f32[4,128]{1,0:T(4,128)S(1)} %dynamic-slice_bitcast_fusion.2, bf16[4,1536,256]{1,2,0:T(8,128)(2,1)} %copy-done.2, f32[4,128,1536]{2,1,0:T(8,128)} %get-tuple-element.165, f32[4,128]{1,0:T(4,128)S(1)} %get-tuple-element.166), kind=kOutput, calls=%fused_computation.43.clone.1 | convolution fusion | flops 106203136 | bytes 13441024 | tf_op jit(solution)/shard_map/while/body/eval_jaxpr/gij,gjd->gid/dot_general | solution.py:100
  314.6 8.7 %fusion.162 = f32[4,1536,64]{1,2,0:T(8,128)} fusion(f32[4,128,1536]{2,1,0:T(8,128)} %fusion.161, f32[4,128]{1,0:T(4,128)S(1)} %dynamic-slice_bitcast_fusion.2, bf16[4,128,128]{2,1,0:T(8,128)(2,1)S(1)} %bitcast.130, f32[4,128,1536]{2,1,0:T(8,128)} %get-tuple-element.165, f32[4,128]{1,0:T(4,128)S(1)} %get-tuple-element.166), kind=kOutput, calls=%fused_computation.29.clone.1 | convolution fusion | flops 106170368 | bytes 14292992 | tf_op jit(solution)/shard_map/while/body/eval_jaxpr/gij,gid->gjd/dot_general | solution.py:103
  326.6 2.8 pad_maximum_fusion.6
  329.4 6.6 %copy.142 = f32[4,1536,256]{2,1,0:T(8,128)} copy(f32[4,1536,256]{1,2,0:T(8,128)} %pad_maximum_fusion.6) | data formatting | bytes 12582912 | tf_op jit(solution)/shard_map/while/body/eval_jaxpr/concatenate | solution.py:109
  336.0 14.8 %scatter_fusion = f32[32,128,256]{2,1,0:T(8,128)} fusion(f32[32,128,256]{2,1,0:T(8,128)} %get-tuple-element.185, s32[48]{0:T(128)S(1)} %fusion.156, f32[48,128,256]{2,1,0:T(8,128)} %bitcast.115), kind=kCustom, calls=%fused_computation.3.clone.1 | custom fusion | flops 1572864 | bytes 18874560 | tf_op jit(solution)/shard_map/while/body/eval_jaxpr/scatter-add | solution.py:112
  358.0 4.7 copy.140
  369.7 3.7 fusion.159
  373.4 7.1 %fusion.166 = bf16[4,128,64]{1,2,0:T(8,128)(2,1)S(1)} fusion(f32[4,128,1536]{2,1,0:T(8,128)} %fusion.163, f32[4,128]{1,0:T(4,128)S(1)} %dynamic-slice_bitcast_fusion.2, bf16[4,1536,256]{1,2,0:T(8,128)(2,1)} %copy-done.2, f32[4,128,1536]{2,1,0:T(8,128)} %get-tuple-element.167, f32[4,128]{1,0:T(4,128)S(1)} %get-tuple-element.168), kind=kOutput, calls=%fused_computation.42.clone.1 | convolution fusion | flops 106203136 | bytes 13441024 | tf_op jit(solution)/shard_map/while/body/eval_jaxpr/gij,gjd->gid/dot_general | solution.py:100
  380.5 8.5 %fusion.164 = f32[4,1536,64]{1,2,0:T(8,128)} fusion(f32[4,128,1536]{2,1,0:T(8,128)} %fusion.163, f32[4,128]{1,0:T(4,128)S(1)} %dynamic-slice_bitcast_fusion.2, bf16[4,128,128]{2,1,0:T(8,128)(2,1)S(1)} %bitcast.128, f32[4,128,1536]{2,1,0:T(8,128)} %get-tuple-element.167, f32[4,128]{1,0:T(4,128)S(1)} %get-tuple-element.168), kind=kOutput, calls=%fused_computation.31.clone.1 | convolution fusion | flops 106170368 | bytes 14292992 | tf_op jit(solution)/shard_map/while/body/eval_jaxpr/gij,gid->gjd/dot_general | solution.py:103
  389.0 3.5 fusion.160
  392.5 3.8 fusion.157
  396.3 7.2 %fusion.165 = bf16[4,128,64]{1,2,0:T(8,128)(2,1)S(1)} fusion(f32[4,128,1536]{2,1,0:T(8,128)} %fusion.161, f32[4,128]{1,0:T(4,128)S(1)} %dynamic-slice_bitcast_fusion.2, bf16[4,1536,256]{1,2,0:T(8,128)(2,1)} %copy-done.2, f32[4,128,1536]{2,1,0:T(8,128)} %get-tuple-element.165, f32[4,128]{1,0:T(4,128)S(1)} %get-tuple-element.166), kind=kOutput, calls=%fused_computation.43.clone.1 | convolution fusion | flops 106203136 | bytes 13441024 | tf_op jit(solution)/shard_map/while/body/eval_jaxpr/gij,gjd->gid/dot_general | solution.py:100
  403.5 8.7 %fusion.162 = f32[4,1536,64]{1,2,0:T(8,128)} fusion(f32[4,128,1536]{2,1,0:T(8,128)} %fusion.161, f32[4,128]{1,0:T(4,128)S(1)} %dynamic-slice_bitcast_fusion.2, bf16[4,128,128]{2,1,0:T(8,128)(2,1)S(1)} %bitcast.130, f32[4,128,1536]{2,1,0:T(8,128)} %get-tuple-element.165, f32[4,128]{1,0:T(4,128)S(1)} %get-tuple-element.166), kind=kOutput, calls=%fused_computation.29.clone.1 | convolution fusion | flops 106170368 | bytes 14292992 | tf_op jit(solution)/shard_map/while/body/eval_jaxpr/gij,gid->gjd/dot_general | solution.py:103
  415.5 2.8 pad_maximum_fusion.6
  418.3 6.6 %copy.142 = f32[4,1536,256]{2,1,0:T(8,128)} copy(f32[4,1536,256]{1,2,0:T(8,128)} %pad_maximum_fusion.6) | data formatting | bytes 12582912 | tf_op jit(solution)/shard_map/while/body/eval_jaxpr/concatenate | solution.py:109
  424.9 14.8 %scatter_fusion = f32[32,128,256]{2,1,0:T(8,128)} fusion(f32[32,128,256]{2,1,0:T(8,128)} %get-tuple-element.185, s32[48]{0:T(128)S(1)} %fusion.156, f32[48,128,256]{2,1,0:T(8,128)} %bitcast.115), kind=kCustom, calls=%fused_computation.3.clone.1 | custom fusion | flops 1572864 | bytes 18874560 | tf_op jit(solution)/shard_map/while/body/eval_jaxpr/scatter-add | solution.py:112
  442.3 16.7 %all_to_all.118 = bf16[16,128,256]{2,1,0:T(8,128)(2,1)S(1)} all-to-all(bf16[16,128,256]{2,1,0:T(8,128)(2,1)S(1)} %slice.109), channel_id=1, replica_groups=mesh['dom'=4,'head'=8] {'dom'}, dimensions={0} | all-to-all | bytes 2097152 | tf_op jit(solution)/shard_map/all_to_all | solution.py:119
  459.0 3.5 all-to-all-start.4
  462.5 4.6 copy.105
  469.0 8.8 %all-to-all-done.4 = bf16[8,256,128]{2,1,0:T(8,128)(2,1)S(1)} async-done(((bf16[8,256,128]{2,1,0:T(8,128)(2,1)}), bf16[8,256,128]{2,1,0:T(8,128)(2,1)S(1)}, u32[]{:S(2)}, u32[]{:S(2)}) %all-to-all-start.4) | async-done | bytes 524320 | tf_op jit(solution)/shard_map/all_to_all | solution.py:129
  477.8 3.5 all-to-all-start.7
  482.2 14.3 %all-to-all-done.7 = bf16[8,256,128]{2,1,0:T(8,128)(2,1)S(1)} async-done(((bf16[8,256,128]{2,1,0:T(8,128)(2,1)}), bf16[8,256,128]{2,1,0:T(8,128)(2,1)S(1)}, u32[]{:S(2)}, u32[]{:S(2)}) %all-to-all-start.7) | async-done | bytes 524320 | tf_op jit(solution)/shard_map/all_to_all | solution.py:131
  496.6 3.5 all-to-all-start.6
  502.5 12.8 %all-to-all-done.6 = bf16[8,256,128]{2,1,0:T(8,128)(2,1)S(1)} async-done(((bf16[8,256,128]{2,1,0:T(8,128)(2,1)}), bf16[8,256,128]{2,1,0:T(8,128)(2,1)S(1)}, u32[]{:S(2)}, u32[]{:S(2)}) %all-to-all-start.6) | async-done | bytes 524320 | tf_op jit(solution)/shard_map/all_to_all | solution.py:130
  (184 shorter events, 93.6 us)
Async XLA Ops:
  0.6 1.1 copy-start
  0.6 20.2 %copy-start.8 = (bf16[256,1024]{1,0:T(8,128)(2,1)S(1)}, bf16[256,1024]{1,0:T(8,128)(2,1)}, u32[]{:S(2)}) copy-start(bf16[256,1024]{1,0:T(8,128)(2,1)} %param.11) | copy-start | bytes 1572868
  2.6 26.4 %copy-start.12 = (s32[2048]{0:T(1024)S(1)}, s32[2048]{0:T(1024)}, u32[]{:S(2)}) copy-start(s32[2048]{0:T(1024)} %param.13) | copy-start | bytes 24580
  2.6 27.1 %copy-start.9 = (bf16[256,1024]{1,0:T(8,128)(2,1)S(1)}, bf16[256,1024]{1,0:T(8,128)(2,1)}, u32[]{:S(2)}) copy-start(bf16[256,1024]{1,0:T(8,128)(2,1)} %param.9) | copy-start | bytes 1572868
  2.6 22.3 %all-to-all-start.1 = ((bf16[256,8,128]{2,0,1:T(8,128)(2,1)}), bf16[256,8,128]{2,0,1:T(8,128)(2,1)S(1)}, u32[]{:S(2)}, u32[]{:S(2)}) async-start(bf16[256,8,128]{2,0,1:T(8,128)(2,1)} %copy_bitcast_fusion.2), calls=%async_computation.1 | async-start | bytes 1048576 | tf_op jit(solution)/shard_map/all_to_all | solution.py:59
  11.1 38.3 %collective-permute-start = (bf16[256,128]{1,0:T(8,128)(2,1)}, bf16[256,128]{1,0:T(8,128)(2,1)}, u32[]{:S(2)}, u32[]{:S(2)}) collective-permute-start(bf16[256,128]{1,0:T(8,128)(2,1)} %bitcast.17), channel_id=1, source_target_pairs={{0,1},{1,0},{2,3},{3,2},{4,5},{5,4},{6,7},{7,6},{8,9},{9,8},{10,11... | collective-permute-start | bytes 196616 | tf_op jit(solution)/shard_map/ppermute | solution.py:51
  12.3 39.3 %collective-permute-start.1 = (bf16[256,128]{1,0:T(8,128)(2,1)}, bf16[256,128]{1,0:T(8,128)(2,1)}, u32[]{:S(2)}, u32[]{:S(2)}) collective-permute-start(bf16[256,128]{1,0:T(8,128)(2,1)} %bitcast.19), channel_id=1, source_target_pairs={{0,2},{1,3},{2,0},{3,1},{4,6},{5,7},{6,4},{7,5},{8,10},{9,11},{10,... | collective-permute-start | bytes 196616 | tf_op jit(solution)/shard_map/ppermute | solution.py:51
  14.1 39.8 %collective-permute-start.2 = (bf16[256,128]{1,0:T(8,128)(2,1)S(1)}, bf16[256,128]{1,0:T(8,128)(2,1)S(1)}, u32[]{:S(2)}, u32[]{:S(2)}) collective-permute-start(bf16[256,128]{1,0:T(8,128)(2,1)S(1)} %bitcast.141), channel_id=1, source_target_pairs={{0,3},{1,2},{2,1},{3,0},{4,7},{5,6},{6,5},{7,4},{8,11},{9,10},{10,... | collective-permute-start | bytes 196616 | tf_op jit(solution)/shard_map/ppermute | solution.py:51
  14.3 52.8 %collective-permute-start.3 = (bf16[256,128]{1,0:T(8,128)(2,1)S(1)}, bf16[256,128]{1,0:T(8,128)(2,1)S(1)}, u32[]{:S(2)}, u32[]{:S(2)}) collective-permute-start(bf16[256,128]{1,0:T(8,128)(2,1)S(1)} %bitcast.140), channel_id=1, source_target_pairs={{0,4},{1,5},{2,6},{3,7},{4,0},{5,1},{6,2},{7,3},{8,12},{9,13},{10,... | collective-permute-start | bytes 196616 | tf_op jit(solution)/shard_map/ppermute | solution.py:51
  17.1 50.0 %collective-permute-start.4 = (bf16[256,128]{1,0:T(8,128)(2,1)S(1)}, bf16[256,128]{1,0:T(8,128)(2,1)S(1)}, u32[]{:S(2)}, u32[]{:S(2)}) collective-permute-start(bf16[256,128]{1,0:T(8,128)(2,1)S(1)} %bitcast.139), channel_id=1, source_target_pairs={{0,5},{1,4},{2,7},{3,6},{4,1},{5,0},{6,3},{7,2},{8,13},{9,12},{10,... | collective-permute-start | bytes 196616 | tf_op jit(solution)/shard_map/ppermute | solution.py:51
  18.1 10.3 %copy-start.13 = (s32[16]{0:T(128)}, s32[16]{0:T(128)S(1)}, u32[]{:S(2)}) copy-start(s32[16]{0:T(128)S(1)} %max.25) | copy-start | bytes 196
  24.9 18.8 %all-to-all-start.2 = ((bf16[256,8,128]{2,0,1:T(8,128)(2,1)}), bf16[256,8,128]{2,0,1:T(8,128)(2,1)S(1)}, u32[]{:S(2)}, u32[]{:S(2)}) async-start(bf16[256,8,128]{2,0,1:T(8,128)(2,1)} %copy_bitcast_fusion.1), calls=%async_computation.2 | async-start | bytes 1048576 | tf_op jit(solution)/shard_map/all_to_all | solution.py:60
  29.0 15.6 %copy-start.15 = (pred[16]{0:T(512)(128)(4,1)S(1)}, pred[16]{0:T(512)(128)(4,1)}, u32[]{:S(2)}) copy-start(pred[16]{0:T(512)(128)(4,1)} %broadcast_compare_fusion) | copy-start | bytes 52
  43.8 5.7 %copy-start.16 = (s32[8]{0:T(128)S(1)}, s32[8]{0:T(128)}, u32[]{:S(2)}) copy-start(s32[8]{0:T(128)} %fusion.90) | copy-start | bytes 100
  44.5 4.9 copy-start.11
  44.6 6.2 %copy-start.7 = (bf16[8,256,128]{2,1,0:T(8,128)(2,1)S(1)}, bf16[8,256,128]{2,1,0:T(8,128)(2,1)}, u32[]{:S(2)}) copy-start(bf16[8,256,128]{2,1,0:T(8,128)(2,1)} %bitcast_dynamic-update-slice_fusion.8) | copy-start | bytes 1572868
  44.6 7.1 %copy-start.10 = (bf16[256,1,128]{2,0,1:T(8,128)(2,1)S(1)}, bf16[256,1,128]{2,0,1:T(8,128)(2,1)}, u32[]{:S(2)}) copy-start(bf16[256,1,128]{2,0,1:T(8,128)(2,1)} %copy.103) | copy-start | bytes 196612
  45.7 17.2 %all-to-all-start.3 = ((bf16[16,128,256]{2,1,0:T(8,128)(2,1)}), bf16[16,128,256]{2,1,0:T(8,128)(2,1)S(1)}, u32[]{:S(2)}, u32[]{:S(2)}) async-start(bf16[16,128,256]{2,1,0:T(8,128)(2,1)} %broadcast_select_fusion.1), calls=%async_computation.3 | async-start | bytes 2097152 | tf_op jit(solution)/shard_map/all_to_all | solution.py:32
  49.5 17.7 %collective-permute-start.5 = (bf16[256,128]{1,0:T(8,128)(2,1)S(1)}, bf16[256,128]{1,0:T(8,128)(2,1)S(1)}, u32[]{:S(2)}, u32[]{:S(2)}) collective-permute-start(bf16[256,128]{1,0:T(8,128)(2,1)S(1)} %bitcast.143), channel_id=1, source_target_pairs={{0,6},{1,7},{2,4},{3,5},{4,2},{5,3},{6,0},{7,1},{8,14},{9,15},{10,... | collective-permute-start | bytes 196616 | tf_op jit(solution)/shard_map/ppermute | solution.py:51
  51.7 15.5 %collective-permute-start.6 = (bf16[256,128]{1,0:T(8,128)(2,1)S(1)}, bf16[256,128]{1,0:T(8,128)(2,1)S(1)}, u32[]{:S(2)}, u32[]{:S(2)}) collective-permute-start(bf16[256,128]{1,0:T(8,128)(2,1)S(1)} %bitcast.142), channel_id=1, source_target_pairs={{0,7},{1,6},{2,5},{3,4},{4,3},{5,2},{6,1},{7,0},{8,15},{9,14},{10,... | collective-permute-start | bytes 196616 | tf_op jit(solution)/shard_map/ppermute | solution.py:51
  62.9 4.3 copy-start.6
  62.9 19.5 %all-to-all-start = ((bf16[256,8,128]{2,0,1:T(8,128)(2,1)}), bf16[256,8,128]{2,0,1:T(8,128)(2,1)}, u32[]{:S(2)}, u32[]{:S(2)}) async-start(bf16[256,8,128]{2,0,1:T(8,128)(2,1)} %copy_bitcast_fusion.3), calls=%async_computation | async-start | bytes 1048576 | tf_op jit(solution)/shard_map/all_to_all | solution.py:58
  98.1 2.6 copy-start.2
  145.5 2.6 copy-start.3
  145.5 2.8 copy-start.4
  145.5 3.3 copy-start.5
  187.1 2.6 copy-start.2
  234.5 2.6 copy-start.3
  234.5 2.8 copy-start.4
  234.5 3.3 copy-start.5
  275.9 2.6 copy-start.2
  323.3 2.6 copy-start.3
  323.3 2.8 copy-start.4
  323.3 3.3 copy-start.5
  364.8 2.6 copy-start.2
  412.2 2.6 copy-start.3
  412.2 2.8 copy-start.4
  412.2 3.3 copy-start.5
  459.0 18.8 %all-to-all-start.4 = ((bf16[8,256,128]{2,1,0:T(8,128)(2,1)}), bf16[8,256,128]{2,1,0:T(8,128)(2,1)S(1)}, u32[]{:S(2)}, u32[]{:S(2)}) async-start(bf16[8,256,128]{2,1,0:T(8,128)(2,1)} %bitcast.33), calls=%async_computation.4 | async-start | bytes 1048576 | tf_op jit(solution)/shard_map/all_to_all | solution.py:129
  462.5 4.6 copy-start.14
  477.8 18.8 %all-to-all-start.7 = ((bf16[8,256,128]{2,1,0:T(8,128)(2,1)}), bf16[8,256,128]{2,1,0:T(8,128)(2,1)S(1)}, u32[]{:S(2)}, u32[]{:S(2)}) async-start(bf16[8,256,128]{2,1,0:T(8,128)(2,1)} %bitcast.41), calls=%async_computation.7 | async-start | bytes 1048576 | tf_op jit(solution)/shard_map/all_to_all | solution.py:131
  496.6 18.8 %all-to-all-start.6 = ((bf16[8,256,128]{2,1,0:T(8,128)(2,1)}), bf16[8,256,128]{2,1,0:T(8,128)(2,1)S(1)}, u32[]{:S(2)}, u32[]{:S(2)}) async-start(bf16[8,256,128]{2,1,0:T(8,128)(2,1)} %bitcast.38), calls=%async_computation.6 | async-start | bytes 1048576 | tf_op jit(solution)/shard_map/all_to_all | solution.py:130
  500.1 16.5 %copy-start.1 = (bf16[256,1024]{1,0:T(8,128)(2,1)S(1)}, bf16[256,1024]{1,0:T(8,128)(2,1)}, u32[]{:S(2)}) copy-start(bf16[256,1024]{1,0:T(8,128)(2,1)} %param.10) | copy-start | bytes 1572868
